TPU v7x, 32 devices: a whole 2x2x4 slice. The times are simulated.
32 devices in a mesh: tm: 8 (over z, x), space: 4 (over y, core).
Axes of the slice: x: 2, y: 2, z: 4, core: 2. Of those that a mesh axis runs over, the one named last changes fastest.
Arguments:
- frames: bfloat16 [32, 16, 128, 128], P('tm', 'space'), may hold values from -6 to 6
- conv_weight: bfloat16 [3456, 128], replicated, may hold values from -0.109375 to 0.109375
- conv_bias: float32 [128], replicated, may hold values from -3 to 3
- projection: float32 [128, 6], replicated, may hold values from -1 to 1
- levels: int32 [6], replicated, may hold values from 3 to 8, as said below
- centres: int32 [8, 16, 768], P(None, 'space', 'tm'), may hold values from 0 to 7, as said below
- code_grad: float32 [8, 16, 768], P(None, 'space', 'tm'), may hold values from -6 to 6
Outputs:
- quantized: float32 [8, 16, 768], P(None, 'space', 'tm')
- weight_grad: float32 [3456, 128], P('tm', 'space')
- projection_grad: float32 [128, 6], replicated
- bias_grad: float32 [128], replicated
Inputs may be any that keep to these rules, and one draw needn't show every extreme that they name: Level counts of the FSQ channels; in every draw some channel has 3 levels and some has 8. centres[g, h, q] is below levels[q % 6].
All inputs are finite; a program needn't handle non-finite values.
Results may differ from a plain program's by a relative error of at most 0.0024.
Values may be sent and summed in bfloat16 or wider, within the bound.
A program may use at most 64 MiB of HBM per device.

v0:
```python
import jax
import jax.numpy as jnp
from jax import lax
from jax.sharding import PartitionSpec as P

offset_scale = 0.45
commit_weight = 0.25
highest = lax.Precision.HIGHEST


def passed_along(value, axis, steps):
    count = lax.axis_size(axis)
    first, last = (max(0, -steps), min(count, count - steps))
    return lax.ppermute(value, axis, [(source, source + steps) for source in range(first, last)])


def extended(block, sides, width):
    for axis, dim in sides:
        count = lax.axis_size(axis)
        forward = [(i, i + 1) for i in range(count - 1)]
        backward = [(target, source) for source, target in forward]
        low = lax.ppermute(
            lax.slice_in_dim(block, block.shape[dim] - width, None, axis=dim), axis, forward
        )
        high = lax.ppermute(lax.slice_in_dim(block, 0, width, axis=dim), axis, backward)
        block = jnp.concatenate([low, block, high], axis=dim)
    return block


def widen_columns(bordered):
    frame_width = bordered.shape[2]
    padded = jnp.pad(bordered, ((0, 0), (0, 0), (1, 1), (0, 0)))
    return jnp.concatenate(
        [padded[:, :, column_shift : column_shift + frame_width] for column_shift in range(3)],
        axis=3,
    )


def tap_slabs(widened, frame_count, row_count):
    triple = widened.shape[3]
    slabs = []
    for time_tap in range(3):
        for row_tap in range(3):
            slabs.append(
                widened[time_tap : time_tap + frame_count, row_tap : row_tap + row_count].reshape(
                    -1, triple
                )
            )
    return slabs


def on_device(frames, conv_weight, conv_bias, projection, levels, centres, code_grad):
    frame_count, row_count, frame_width, channels = frames.shape
    first_device = lax.axis_index("tm") == 0
    received = passed_along(frames[frame_count - 2 :], "tm", 1)
    earlier = jnp.where(first_device, jnp.broadcast_to(frames[:1], received.shape), received)
    bordered = extended(jnp.concatenate([earlier, frames], 0), (("space", 1),), 1)
    slabs = tap_slabs(widen_columns(bordered), frame_count, row_count)
    triple = 3 * channels
    cell_count = row_count * frame_width
    preact = jnp.zeros((frame_count * cell_count, channels), jnp.float32) + conv_bias
    for tap_number in range(9):
        preact = preact + jnp.dot(
            slabs[tap_number],
            conv_weight[tap_number * triple : (tap_number + 1) * triple],
            preferred_element_type=jnp.float32,
        )
    activated = lax.optimization_barrier(jax.nn.silu(preact).astype(jnp.bfloat16))
    group_count = frame_count // 4
    pooled = (
        activated.astype(jnp.float32).reshape(group_count, 4, cell_count, channels).sum(1) * 0.25
    )
    latent_count = levels.shape[0]
    latent = jnp.dot(pooled, projection, precision=highest).reshape(
        group_count, row_count, frame_width * latent_count
    )
    tiled_latent = lax.all_to_all(latent, "tm", split_axis=2, concat_axis=0, tiled=True)
    half_range = (levels.astype(jnp.float32) - 1.0) * 0.5
    half_column = jnp.tile(half_range, tiled_latent.shape[2] // latent_count)
    quantized = (centres.astype(jnp.float32) - half_column) / half_column
    squashed = jnp.tanh(tiled_latent)
    total_cells = 4 * tiled_latent.shape[0] * row_count * lax.axis_size("space") * frame_width
    tile_step = (
        (code_grad / half_column + 2.0 * commit_weight * offset_scale * squashed)
        * offset_scale
        * (1.0 - squashed * squashed)
        * float(total_cells) ** (-0.5)
    )
    code_step = lax.all_to_all(tile_step, "tm", split_axis=0, concat_axis=2, tiled=True).reshape(
        group_count, cell_count, latent_count
    )
    projection_part = jnp.einsum("gnc,gnl->cl", pooled, code_step, precision=highest)
    pooled_grad = jnp.dot(code_step, projection.T, precision=highest)
    sigmoid_pre = jax.nn.sigmoid(preact)
    silu_slope = sigmoid_pre * (1.0 + preact * (1.0 - sigmoid_pre))
    pre_grad = (
        0.25 * pooled_grad[:, None] * silu_slope.reshape(group_count, 4, cell_count, channels)
    ).reshape(-1, channels)
    bias_part = pre_grad.sum(0)
    low_grad = pre_grad.astype(jnp.bfloat16)
    weight_sum = jnp.concatenate(
        [
            lax.dot_general(
                tap_slab, low_grad, (((0,), (0,)), ((), ())), preferred_element_type=jnp.float32
            )
            for tap_slab in slabs
        ],
        0,
    )
    column_part = lax.psum_scatter(weight_sum, "space", scatter_dimension=1, tiled=True)
    weight_grad = lax.psum_scatter(column_part, "tm", scatter_dimension=0, tiled=True)
    projection_grad, bias_grad = lax.psum((projection_part, bias_part), ("tm", "space"))
    return (quantized, weight_grad, projection_grad, bias_grad)


def solution(mesh):
    return jax.shard_map(
        on_device,
        mesh=mesh,
        in_specs=(
            P("tm", "space", None, None),
            P(),
            P(),
            P(),
            P(),
            P(None, "space", "tm"),
            P(None, "space", "tm"),
        ),
        out_specs=(P(None, "space", "tm"), P("tm", "space"), P(), P()),
        check_vma=False,
    )
```

profile of v0, /device:TPU:24, one launch (start us, length us, event | category | flops | bytes accessed | tf_op | source)
XLA Modules:
  0.0 195.5 jit_solution(2224185399356054323)
XLA Ops:
  8.2 3.4 %collective-permute-start = (bf16[2,4,128,128]{3,2,1,0:T(8,128)(2,1)S(1)}, bf16[2,4,128,128]{3,2,1,0:T(8,128)(2,1)S(1)}, u32[]{:S(2)}, u32[]{:S(2)}) collective-permute-start(bf16[2,4,128,128]{3,2,1,0:T(8,128)(2,1)S(1)} %slice.74), channel_id=1, source_target_pairs={{0,4},{4,8},{8,12},{12,16},{16,20},{20,24},{24,28},{1,5},{5,9},{9,... | collective-permute-start | bytes 786440 | tf_op jit(solution)/shard_map/ppermute | solution.py:14
  12.6 6.5 %collective-permute-done = bf16[2,4,128,128]{3,2,1,0:T(8,128)(2,1)S(1)} collective-permute-done((bf16[2,4,128,128]{3,2,1,0:T(8,128)(2,1)S(1)}, bf16[2,4,128,128]{3,2,1,0:T(8,128)(2,1)S(1)}, u32[]{:S(2)}, u32[]{:S(2)}) %collective-permute-start) | collective-permute-done | bytes 262176 | tf_op jit(solution)/shard_map/ppermute | solution.py:14
  19.1 1.3 collective-permute-start.1
  20.5 1.3 collective-permute-start.2
  21.8 3.8 %collective-permute-done.2 = bf16[6,1,128,128]{3,2,1,0:T(8,128)(2,1)S(1)} collective-permute-done((bf16[6,1,128,128]{3,2,1,0:T(8,128)(2,1)S(1)}, bf16[6,1,128,128]{3,2,1,0:T(8,128)(2,1)S(1)}, u32[]{:S(2)}, u32[]{:S(2)}) %collective-permute-start.2) | collective-permute-done | bytes 196640 | tf_op jit(solution)/shard_map/ppermute | solution.py:25
  27.3 2.7 %fusion.42 = (bf16[4,4,128,384]{3,2,1,0:T(8,128)(2,1)S(1)}, bf16[4,4,128,384]{3,2,1,0:T(8,128)(2,1)S(1)}, bf16[4,4,128,384]{3,2,1,0:T(8,128)(2,1)S(1)}, bf16[4,4...) fusion(bf16[6,6,128,384]{3,2,1,0:T(8,128)(2,1)S(1)} %pad_maximu, ...), kind=kLoop, calls=%fused_computation.73 | loop fusion | bytes 28311552 | tf_op jit(solution)/shard_map/slice | solution.py:45
  34.9 1.9 multiply_convert_fusion
  38.0 1.1 reshape.101
  40.7 3.4 %reduce.1 = f32[768,4]{1,0:T(8,128)} reduce(f32[768,1,4]{2,1,0:T(1,128)} %bitcast.91, f32[]{:T(128)} %broadcast.60), dimensions={1}, to_apply=%bitcast.36.reduce_sub_computation | reduce | bytes 24580
  44.1 1.9 reshape.109
  45.9 5.1 %all-to-all-start = ((f32[8,1,384]{2,1,0:T(1,128)}), f32[8,1,384]{2,1,0:T(1,128)S(1)}, u32[]{:S(2)}, u32[]{:S(2)}) async-start(f32[8,1,384]{2,1,0:T(1,128)} %reshape.109), calls=%async_computation | async-start | bytes 24576 | tf_op jit(solution)/shard_map/all_to_all | solution.py:77
  51.1 3.2 %all-to-all-done = f32[8,1,384]{2,1,0:T(1,128)S(1)} async-done(((f32[8,1,384]{2,1,0:T(1,128)}), f32[8,1,384]{2,1,0:T(1,128)S(1)}, u32[]{:S(2)}, u32[]{:S(2)}) %all-to-all-start) | async-done | bytes 12320 | tf_op jit(solution)/shard_map/all_to_all | solution.py:77
  55.0 1.4 reshape.110
  56.4 1.1 copy.31
  57.8 8.9 %all_to_all.24 = f32[8,4,96]{2,1,0:T(4,128)S(1)} all-to-all(f32[8,4,96]{2,1,0:T(4,128)S(1)} %copy.32), channel_id=1, replica_groups=mesh['tm'=8,'space'=4] {'tm'}, dimensions={0} | all-to-all | bytes 24576 | tf_op jit(solution)/shard_map/all_to_all | solution.py:89
  67.6 1.4 convolution_multiply_fusion
  69.0 1.7 fusion.41
  70.7 1.3 convolution_dynamic-update-slice_fusion.8
  72.1 1.3 convolution_dynamic-update-slice_fusion.7
  73.5 1.3 convolution_dynamic-update-slice_fusion.6
  75.0 1.3 convolution_dynamic-update-slice_fusion.5
  76.4 1.3 convolution_dynamic-update-slice_fusion.4
  77.8 1.3 convolution_dynamic-update-slice_fusion.3
  79.2 1.3 convolution_dynamic-update-slice_fusion.2
  80.5 1.3 convolution_dynamic-update-slice_fusion.1
  81.8 1.3 convolution_dynamic-update-slice_fusion
  83.0 2.7 %copy.37 = f32[3456,128]{0,1:T(8,128)} copy(f32[3456,128]{1,0:T(8,128)} %convolution_dynamic-update-slice_fusion) | data formatting | bytes 3538944
  85.8 31.7 %reduce-scatter.7.cloned.1.call-done = f32[32,3456]{1,0:T(8,128)} async-done(((f32[128,3456]{1,0:T(8,128)}), f32[32,3456]{1,0:T(8,128)}) %reduce-scatter.7.cloned.1.call-update) | async-done | bytes 442384
  117.6 2.8 %copy.38 = f32[3456,32]{1,0:T(8,128)} copy(f32[3456,32]{0,1:T(8,128)} %bitcast.92) | data formatting | bytes 884736
  121.6 38.7 %all-reduce.1 = (f32[128,6]{0,1:T(8,128)}, f32[128]{0:T(128)}) all-reduce(f32[128,6]{0,1:T(8,128)S(1)} %fusion.12, f32[128]{0:T(128)S(1)} %get-tuple-element.22), channel_id=1, replica_groups=mesh['tm'=8,'space'=4] {'tm','space'}, use_global_device_ids=true, to_apply=%region_3.4 | all-reduce | flops 896 | bytes 7168 | tf_op jit(solution)/shard_map/psum | solution.py:112
  160.3 26.6 %reduce-scatter.5.cloned.1.call-done = f32[432,32]{1,0:T(8,128)} async-done(((f32[3456,32]{1,0:T(8,128)}), f32[432,32]{1,0:T(8,128)}) %reduce-scatter.5.cloned.1.call-update) | async-done | bytes 55312 | tf_op jit(solution)/shard_map/reduce_scatter | solution.py:111
  187.0 1.7 copy.35
  (81 shorter events, 14.9 us)
Async XLA Ops:
  7.2 29.8 %copy-start = (f32[128,6]{0,1:T(8,128)S(1)}, f32[128,6]{0,1:T(8,128)}, u32[]{:S(2)}) copy-start(f32[128,6]{0,1:T(8,128)} %param.10) | copy-start | bytes 9220
  7.2 11.9 %copy-start.15 = (bf16[4,4,128,128]{3,2,1,0:T(8,128)(2,1)S(1)}, bf16[4,4,128,128]{3,2,1,0:T(8,128)(2,1)}, u32[]{:S(2)}) copy-start(bf16[4,4,128,128]{3,2,1,0:T(8,128)(2,1)} %param.7) | copy-start | bytes 1572868
  8.2 10.8 %collective-permute-start = (bf16[2,4,128,128]{3,2,1,0:T(8,128)(2,1)S(1)}, bf16[2,4,128,128]{3,2,1,0:T(8,128)(2,1)S(1)}, u32[]{:S(2)}, u32[]{:S(2)}) collective-permute-start(bf16[2,4,128,128]{3,2,1,0:T(8,128)(2,1)S(1)} %slice.74), channel_id=1, source_target_pairs={{0,4},{4,8},{8,12},{12,16},{16,20},{20,24},{24,28},{1,5},{5,9},{9,... | collective-permute-start | bytes 786440 | tf_op jit(solution)/shard_map/ppermute | solution.py:14
  19.1 2.6 %collective-permute-start.1 = (bf16[6,1,128,128]{3,2,1,0:T(8,128)(2,1)S(1)}, bf16[6,1,128,128]{3,2,1,0:T(8,128)(2,1)S(1)}, u32[]{:S(2)}, u32[]{:S(2)}) collective-permute-start(bf16[6,1,128,128]{3,2,1,0:T(8,128)(2,1)S(1)} %get-tuple-element.35), channel_id=1, source_target_pairs={{0,1},{1,2},{2,3},{4,5},{5,6},{6,7},{8,9},{9,10},{10,11},{12,13},{... | collective-permute-start | bytes 589832 | tf_op jit(solution)/shard_map/ppermute | solution.py:22
  20.5 5.1 %collective-permute-start.2 = (bf16[6,1,128,128]{3,2,1,0:T(8,128)(2,1)S(1)}, bf16[6,1,128,128]{3,2,1,0:T(8,128)(2,1)S(1)}, u32[]{:S(2)}, u32[]{:S(2)}) collective-permute-start(bf16[6,1,128,128]{3,2,1,0:T(8,128)(2,1)S(1)} %get-tuple-element.36), channel_id=1, source_target_pairs={{1,0},{2,1},{3,2},{5,4},{6,5},{7,6},{9,8},{10,9},{11,10},{13,12},{... | collective-permute-start | bytes 589832 | tf_op jit(solution)/shard_map/ppermute | solution.py:25
  27.3 2.8 %copy-start.17 = (bf16[3456,128]{1,0:T(8,128)(2,1)S(1)}, bf16[3456,128]{1,0:T(8,128)(2,1)}, u32[]{:S(2)}) copy-start(bf16[3456,128]{1,0:T(8,128)(2,1)} %param.8) | copy-start | bytes 2654212
  30.1 1.2 copy-start.1
  30.1 1.8 copy-start.3
  30.1 2.4 %copy-start.5 = (bf16[4,4,128,384]{3,2,1,0:T(8,128)(2,1)}, bf16[4,4,128,384]{3,2,1,0:T(8,128)(2,1)S(1)}, u32[]{:S(2)}) copy-start(bf16[4,4,128,384]{3,2,1,0:T(8,128)(2,1)S(1)} %get-tuple-element.29) | copy-start | bytes 4718596
  30.1 3.0 %copy-start.7 = (bf16[4,4,128,384]{3,2,1,0:T(8,128)(2,1)}, bf16[4,4,128,384]{3,2,1,0:T(8,128)(2,1)S(1)}, u32[]{:S(2)}) copy-start(bf16[4,4,128,384]{3,2,1,0:T(8,128)(2,1)S(1)} %get-tuple-element.30) | copy-start | bytes 4718596
  30.1 3.6 %copy-start.9 = (bf16[4,4,128,384]{3,2,1,0:T(8,128)(2,1)}, bf16[4,4,128,384]{3,2,1,0:T(8,128)(2,1)S(1)}, u32[]{:S(2)}) copy-start(bf16[4,4,128,384]{3,2,1,0:T(8,128)(2,1)S(1)} %get-tuple-element.31) | copy-start | bytes 4718596
  30.1 4.1 %copy-start.11 = (bf16[4,4,128,384]{3,2,1,0:T(8,128)(2,1)}, bf16[4,4,128,384]{3,2,1,0:T(8,128)(2,1)S(1)}, u32[]{:S(2)}) copy-start(bf16[4,4,128,384]{3,2,1,0:T(8,128)(2,1)S(1)} %get-tuple-element.24) | copy-start | bytes 4718596
  30.2 4.7 %copy-start.13 = (bf16[4,4,128,384]{3,2,1,0:T(8,128)(2,1)}, bf16[4,4,128,384]{3,2,1,0:T(8,128)(2,1)S(1)}, u32[]{:S(2)}) copy-start(bf16[4,4,128,384]{3,2,1,0:T(8,128)(2,1)S(1)} %get-tuple-element.32) | copy-start | bytes 4718596
  34.3 0.7 copy-start.20
  36.9 14.2 %copy-start.21 = (s32[6]{0:T(128)S(1)}, s32[6]{0:T(128)}, u32[]{:S(2)}) copy-start(s32[6]{0:T(128)} %param.11) | copy-start | bytes 76
  36.9 20.8 %copy-start.18 = (f32[8,4,96]{2,1,0:T(4,128)S(1)}, f32[8,4,96]{2,1,0:T(4,128)}, u32[]{:S(2)}) copy-start(f32[8,4,96]{2,1,0:T(4,128)} %param.13) | copy-start | bytes 36868
  37.0 20.8 %copy-start.19 = (s32[8,4,96]{2,1,0:T(4,128)S(1)}, s32[8,4,96]{2,1,0:T(4,128)}, u32[]{:S(2)}) copy-start(s32[8,4,96]{2,1,0:T(4,128)} %param.12) | copy-start | bytes 36868
  45.9 8.4 %all-to-all-start = ((f32[8,1,384]{2,1,0:T(1,128)}), f32[8,1,384]{2,1,0:T(1,128)S(1)}, u32[]{:S(2)}, u32[]{:S(2)}) async-start(f32[8,1,384]{2,1,0:T(1,128)} %reshape.109), calls=%async_computation | async-start | bytes 24576 | tf_op jit(solution)/shard_map/all_to_all | solution.py:77
  51.0 66.5 %reduce-scatter.7.cloned.1.call-start = ((), (), s32[]{:S(2)}) async-start(), calls=%async_computation.5 | async-start | bytes 2211840
  67.6 3.1 %copy-start.14 = (bf16[4,4,128,384]{3,2,1,0:T(8,128)(2,1)S(1)}, bf16[4,4,128,384]{3,2,1,0:T(8,128)(2,1)}, u32[]{:S(2)}) copy-start(bf16[4,4,128,384]{3,2,1,0:T(8,128)(2,1)} %copy-done.13) | copy-start | bytes 4718596
  70.7 1.4 copy-start.12
  72.1 1.4 copy-start.10
  73.5 1.4 copy-start.8
  75.0 1.4 copy-start.6
  76.4 1.4 copy-start.4
  77.8 1.4 copy-start.2
  85.8 101.2 %reduce-scatter.5.cloned.1.call-start = ((), (), s32[]{:S(2)}) async-start(), calls=%async_computation.4 | async-start | bytes 1990656 | tf_op jit(solution)/shard_map/reduce_scatter | solution.py:111
  117.6 3.5 %copy-start.16 = (f32[512,6]{1,0:T(8,128)S(1)}, f32[512,6]{1,0:T(8,128)}, u32[]{:S(2)}) copy-start(f32[512,6]{1,0:T(8,128)} %reshape.102) | copy-start | bytes 36868
Sparse Core Ops, SparseCore 0:
  85.9 31.6 reduce-scatter.6
  121.0 65.9 reduce-scatter.4
where the time goes:
time: 199 us; the launch traced here: 195 us
  waiting for transfers between devices  71.8 us (36%)
  blocking collectives  47.7 us (24%)
  local copies, waits for them, and re-layouts  22.2 us (11%)
  matrix products  21.2 us (11%)
  between operations  14.4 us (7%)
  starting transfers between devices  11.2 us (6%)
  other arithmetic  7.03 us (4%)
    psum x1, blocking collectives, on_device(): lax.psum((projection_part, bias_part), ('tm', 'space'))  38.7 us
    unnamed x3, waiting for transfers between devices  31.8 us
    reduce_scatter x1, waiting for transfers between devices, on_device(): lax.psum_scatter(column_part, 'tm', scatter_dimension=0, tiled=True)  26.6 us
    unnamed x51, local copies, waits for them, and re-layouts  12.4 us
    dot_general x9, matrix products, on_device(): lax.dot_general(tap_slab, low_grad, (((0,), (0,)), ((), ())), preferred_e...  11.7 us
    all_to_all x1, blocking collectives, on_device(): lax.all_to_all(tile_step, 'tm', split_axis=0, concat_axis=2, tiled=True)  8.94 us
    ppermute x1, waiting for transfers between devices, passed_along(): lax.ppermute(value, axis, [(source, source + steps) for source in range(f...  6.51 us
    dot_general x9, matrix products, on_device(): jnp.dot(slabs[tap_number], conv_weight[tap_number * triple:(tap_number +...  6.5 us
  transfers between devices with their start and end apart: 6, of which 5 were waited for; matrix products, arithmetic and copies ran while one was open for 1% of the time, Pallas kernels for 0%

commit v1 on v0

v1 whole, which is shorter than its diff:
```python
import functools

import jax
import jax.numpy as jnp
from jax import lax
from jax.experimental import pallas as pl
from jax.experimental.pallas import tpu as pltpu
from jax.sharding import PartitionSpec as P

offset_scale = 0.45
commit_weight = 0.25
highest = lax.Precision.HIGHEST
MESH = pl.DeviceIdType.MESH
f32, bf16 = jnp.float32, jnp.bfloat16


def dot(a, b, ca, cb, precision=None):
    return lax.dot_general(
        a, b, (((ca,), (cb,)), ((), ())), preferred_element_type=f32, precision=precision
    )


def per_level(levels_ref, index, count):
    half = jnp.ones(index.shape, f32)
    for j in range(count):
        half = jnp.where(index == j, (levels_ref[j].astype(f32) - 1.0) * 0.5, half)
    return half


def block_kernel(
    T, S, scale,
    frames, weight, bias, proj, levels, centres, code_grad,
    quant_out, weight_out, small_out,
    xb, cg_send, cg_recv, pscr, slope_t, gt, acc, stage1, recv1, sum2, stage2, recv2,
    total, own3, stage3, recv3, sm_send, sm_recv, st_send, st_recv,
    local_sem, halo_s, halo_r, cg_s, cg_r, ss_s, ss_r, ts_s, ts_r,
    core_s, core_r, y_s, y_r, tm_s, tm_r,
):
    Y = S // 2
    F, R, W, C = frames.shape
    L = levels.shape[0]
    TILE = code_grad.shape[2]
    oc = C // S
    KC = weight.shape[0]
    KA = KC // 3
    KT = KC // T
    KTP = stage3.shape[2]
    cells = R * W
    t = lax.axis_index("tm")
    s = lax.axis_index("space")
    y, core = s // 2, s % 2
    up_t, dn_t, up_s, dn_s = t < T - 1, t > 0, s < S - 1, s > 0

    barrier = pltpu.get_barrier_semaphore()

    def signal(tt, ss):
        pl.semaphore_signal(barrier, inc=1, device_id=(tt, ss), device_id_type=MESH)

    for d in range(1, S):
        signal(t, lax.rem(s + d, S))
    for d in range(1, T):
        signal(lax.rem(t + d, T), s)
    for ct, dt in ((up_t, 1), (dn_t, -1)):
        for cs_, ds in ((up_s, 1), (dn_s, -1)):
            @pl.when(jnp.logical_and(ct, cs_))
            def _():
                signal(t + dt, s + ds)

    own = pltpu.make_async_copy(frames, xb.at[2 : 2 + F, 1 : 1 + R], local_sem.at[0])
    own.start()
    first = [
        pltpu.make_async_copy(frames.at[0], xb.at[k, 1 : 1 + R], local_sem.at[1 + k])
        for k in range(2)
    ]

    @pl.when(t == 0)
    def _():
        for copy in first:
            copy.start()

    cg_send[...] = jnp.zeros_like(cg_send)
    cg_send[:, 0:R, 0:TILE] = code_grad[...]

    def diag(cond, dt, ds):
        return jnp.where(cond, 1, 0)

    n_t = jnp.where(up_t, 1, 0) + jnp.where(dn_t, 1, 0)
    n_s = jnp.where(up_s, 1, 0) + jnp.where(dn_s, 1, 0)
    pl.semaphore_wait(barrier, (S - 1) + (T - 1) + n_t * n_s)

    def remote(src, dst, ss_, rs_, tt, sp):
        return pltpu.make_async_remote_copy(
            src_ref=src, dst_ref=dst, send_sem=ss_, recv_sem=rs_,
            device_id=(tt, sp), device_id_type=MESH,
        )

    H = R + 1
    halos = [
        (up_s, dn_s, remote(frames.at[:, R - 1], xb.at[2 : 2 + F, 0],
                            halo_s.at[0], halo_r.at[0], t, s + 1)),
        (dn_s, up_s, remote(frames.at[:, 0], xb.at[2 : 2 + F, H],
                            halo_s.at[1], halo_r.at[1], t, s - 1)),
        (up_t, dn_t, remote(frames.at[F - 2 : F], xb.at[0:2, 1:H],
                            halo_s.at[2], halo_r.at[2], t + 1, s)),
        (jnp.logical_and(up_t, up_s), jnp.logical_and(dn_t, dn_s),
         remote(frames.at[F - 2 : F, R - 1], xb.at[0:2, 0],
                halo_s.at[3], halo_r.at[3], t + 1, s + 1)),
        (jnp.logical_and(up_t, dn_s), jnp.logical_and(dn_t, up_s),
         remote(frames.at[F - 2 : F, 0], xb.at[0:2, H],
                halo_s.at[4], halo_r.at[4], t + 1, s - 1)),
    ]

    def start_if(cond, copy):
        @pl.when(cond)
        def _():
            copy.start()

    def recv_if(cond, copy):
        @pl.when(cond)
        def _():
            copy.wait_recv()

    def sent_if(cond, copy):
        @pl.when(cond)
        def _():
            copy.wait_send()

    for sends, _, copy in halos:
        start_if(sends, copy)

    def cg_copy(d):
        to = lax.rem(t + d, T)
        return remote(cg_send.at[to], cg_recv.at[d], cg_s.at[d], cg_r.at[d], to, s)

    for d in range(1, T):
        cg_copy(d).start()

    lane3 = lax.broadcasted_iota(jnp.int32, centres.shape, 2)
    half3 = per_level(levels, lax.rem(lane3, L), L)
    quant_out[...] = (centres[...].astype(f32) - half3) / half3

    pscr[...] = jnp.zeros_like(pscr)
    pscr[:, 0:L] = proj[...]
    proj_t = pscr[...].T[0:8]

    @pl.when(s == 0)
    def _():
        xb[:, 0] = jnp.zeros((F + 2, W, C), bf16)

    @pl.when(s == S - 1)
    def _():
        xb[:, H] = jnp.zeros((F + 2, W, C), bf16)

    row = lax.broadcasted_iota(jnp.int32, (cells, C), 0) % W

    def conv_frame(f):
        slabs = []
        weights = []
        for a in range(3):
            for b in range(3):
                slabs.append(xb[f + a, b : b + R].reshape(cells, C))
                k0 = (a * 3 + b) * 3 * C
                weights.append(
                    jnp.concatenate([weight[k0 + c * C : k0 + (c + 1) * C] for c in range(3)], 1)
                )
        out = dot(jnp.concatenate(slabs, 1), jnp.concatenate(weights, 0), 1, 0)
        left = jnp.where(row == 0, 0.0, pltpu.roll(out[:, 0:C], 1, 0))
        right = jnp.where(row == W - 1, 0.0, pltpu.roll(out[:, 2 * C :], cells - 1, 0))
        pre = out[:, C : 2 * C] + bias[...] + left + right
        sig = 1.0 / (1.0 + jnp.exp(-pre))
        act = (pre * sig).astype(bf16).astype(f32)
        slope = sig * (1.0 + pre * (1.0 - sig))
        for h in range(R):
            slope_t[f * R + h] = slope[h * W : (h + 1) * W].T
        return act

    own.wait()
    for _, gets, copy in halos[:2]:
        recv_if(gets, copy)
    pooled = conv_frame(2) + conv_frame(3)

    for _, gets, copy in halos[2:]:
        recv_if(gets, copy)

    @pl.when(t == 0)
    def _():
        for k in range(2):
            first[k].wait()
            xb[k, 0] = xb[2, 0]
            xb[k, H] = xb[2, H]

    pooled = (pooled + conv_frame(0) + conv_frame(1)) * 0.25

    for d in range(1, T):
        cg_copy(d).wait_recv()
    wt = TILE // L
    mine = cg_send[pl.ds(t, 1)]
    pieces = [mine]
    for d in range(1, T):
        pieces.append(cg_recv[d : d + 1])
    cg_all = jnp.concatenate(pieces, 0).reshape(T * 8, 128)
    r_i = lax.broadcasted_iota(jnp.int32, (T * 8, cells), 0)
    q_i = lax.broadcasted_iota(jnp.int32, (T * 8, cells), 1)
    owner = lax.rem(t - r_i // 8 + T, T)
    pick = jnp.logical_and(r_i % 8 == q_i // W, owner == (q_i % W) // wt).astype(f32)
    spread = dot(cg_all, pick, 0, 0, highest)
    l_i = lax.broadcasted_iota(jnp.int32, (128, cells), 0)
    w_i = lax.broadcasted_iota(jnp.int32, (128, cells), 1) % W
    spread = jnp.where(jnp.logical_and(l_i // L == w_i % wt, l_i < TILE), spread, 0.0)
    j_i = lax.broadcasted_iota(jnp.int32, (8, 128), 0)
    m_i = lax.broadcasted_iota(jnp.int32, (8, 128), 1)
    fold = jnp.logical_and(m_i % L == j_i, m_i < TILE).astype(f32)
    code = dot(fold, spread, 1, 0, highest)

    latent = dot(proj_t, pooled, 1, 1, highest)
    squashed = jnp.tanh(latent)
    half_j = per_level(levels, lax.broadcasted_iota(jnp.int32, (8, cells), 0), L)
    step = (
        (code / half_j + 2.0 * commit_weight * offset_scale * squashed)
        * offset_scale
        * (1.0 - squashed * squashed)
        * scale
    )
    proj_part = dot(step, pooled, 1, 0, highest)
    pg_t = dot(pscr[:, 0:8], step, 1, 0, highest) * 0.25

    lane = lax.broadcasted_iota(jnp.int32, (C, W), 1)
    bias_sum = jnp.zeros((C, W), f32)
    for f in range(F):
        for h in range(R):
            g = pg_t[:, h * W : (h + 1) * W] * slope_t[f * R + h]
            bias_sum = bias_sum + g
            q0 = (f * R + h) * W
            gt[0:C, q0 : q0 + W] = jnp.where(lane == W - 1, 0.0, pltpu.roll(g, W - 1, 1)).astype(bf16)
            gt[C : 2 * C, q0 : q0 + W] = g.astype(bf16)
            gt[2 * C :, q0 : q0 + W] = jnp.where(lane == 0, 0.0, pltpu.roll(g, 1, 1)).astype(bf16)
    bias_part = dot(jnp.ones((8, W), f32), bias_sum, 1, 1, highest)
    sm_send[...] = jnp.where(lax.broadcasted_iota(jnp.int32, (8, C), 0) == L, bias_part, proj_part)

    def small_space(d):
        return remote(sm_send, sm_recv.at[d], ss_s.at[d], ss_r.at[d], t, lax.rem(s + d, S))

    def small_time(d):
        return remote(st_send, st_recv.at[d], ts_s.at[d], ts_r.at[d], lax.rem(t + d, T), s)

    for d in range(1, S):
        small_space(d).start()

    def core_copy(a):
        return remote(stage1.at[a, 1 - core], recv1.at[a], core_s.at[a], core_r.at[a], t, s + 1 - 2 * core)

    def y_copy(a, d):
        to = lax.rem(y + d, Y)
        return remote(stage2.at[a, to], recv2.at[a, d], y_s.at[a, d], y_r.at[a, d], t, to * 2 + core)

    def tm_copy(to, slot):
        return remote(stage3.at[to], recv3.at[slot], tm_s.at[to], tm_r.at[slot], to, s)

    def products(a):
        rhs = jnp.concatenate(
            [xb[a : a + F, b : b + R].reshape(F * cells, C) for b in range(3)], 1
        )
        res = dot(gt[...], rhs, 1, 0)
        for b in range(3):
            for c in range(3):
                k0 = (b * 3 + c) * C
                for sp in range(S):
                    blk = res[c * C + sp * oc : c * C + (sp + 1) * oc, b * C : (b + 1) * C]
                    acc[a, sp % 2, sp // 2, :, k0 : k0 + C] = blk
                    stage1[a, sp % 2, sp // 2, :, k0 : k0 + C] = blk.astype(bf16)
        core_copy(a).start()

    def fold_core(a):
        core_copy(a).wait_recv()
        for yy in range(Y):
            v = acc[a, core, yy] + recv1[a, yy].astype(f32)
            sum2[a, yy] = v
            stage2[a, yy] = v.astype(bf16)
        for d in range(1, Y):
            y_copy(a, d).start()

    done = [0]

    def fold_y(a):
        v = sum2[a, y]
        for d in range(1, Y):
            y_copy(a, d).wait_recv()
            v = v + recv2[a, d].astype(f32)
        total[:, a * KA : (a + 1) * KA] = v
        while (done[0] + 1) * KT <= (a + 1) * KA:
            to = done[0]
            off = to * KT
            base = off // 128 * 128
            win = total[:, base : base + KTP + 128]
            if off > base:
                win = pltpu.roll(win, KTP + 128 - (off - base), 1)
            win = win[:, 0:KTP]
            own3[to] = win
            stage3[to] = win.astype(bf16)
            start_if(t != to, tm_copy(to, t))
            done[0] += 1

    total[:, KC:] = jnp.zeros((oc, total.shape[1] - KC), f32)
    products(0)
    sm = sm_send[...]
    for d in range(1, S):
        small_space(d).wait_recv()
        sm = sm + sm_recv[d]
    st_send[...] = sm
    for d in range(1, T):
        small_time(d).start()
    products(1)
    fold_core(0)
    products(2)
    fold_core(1)
    fold_y(0)
    fold_core(2)
    fold_y(1)
    fold_y(2)

    for d in range(1, T):
        small_time(d).wait_recv()
        sm = sm + st_recv[d]
    small_out[...] = sm

    res = own3[t]
    for d in range(1, T):
        src = lax.rem(t + d, T)
        tm_copy(src, src).wait_recv()
        res = res + recv3[src].astype(f32)
    weight_out[...] = res

    for sends, _, copy in halos:
        sent_if(sends, copy)
    for d in range(1, T):
        cg_copy(d).wait_send()
        small_time(d).wait_send()
    for d in range(1, S):
        small_space(d).wait_send()
    for a in range(3):
        core_copy(a).wait_send()
        for d in range(1, Y):
            y_copy(a, d).wait_send()
    for to in range(T):
        sent_if(t != to, tm_copy(to, t))


def on_device(T, S, frames, conv_weight, conv_bias, projection, levels, centres, code_grad):
    F, R, W, C = frames.shape
    KC = conv_weight.shape[0]
    KT = KC // T
    KTP = -(-KT // 128) * 128
    oc, Y, cells = C // S, S // 2, R * W
    scale = float(F * T * R * S * W) ** -0.5
    vmem = pl.BlockSpec(memory_space=pltpu.VMEM)
    dma = pltpu.SemaphoreType.DMA
    KA = KC // 3
    quantized, wg, small = pl.pallas_call(
        functools.partial(block_kernel, T, S, scale),
        out_shape=(
            jax.ShapeDtypeStruct(centres.shape, f32),
            jax.ShapeDtypeStruct((oc, KTP), f32),
            jax.ShapeDtypeStruct((8, C), f32),
        ),
        in_specs=[
            pl.BlockSpec(memory_space=pl.ANY), vmem, vmem, vmem,
            pl.BlockSpec(memory_space=pltpu.SMEM), vmem, vmem,
        ],
        out_specs=(vmem, vmem, vmem),
        scratch_shapes=[
            pltpu.VMEM((F + 2, R + 2, W, C), bf16),
            pltpu.VMEM((T, 8, 128), f32),
            pltpu.VMEM((T, 8, 128), f32),
            pltpu.VMEM((C, C), f32),
            pltpu.VMEM((F * R, C, W), f32),
            pltpu.VMEM((3 * C, F * cells), bf16),
            pltpu.VMEM((3, 2, Y, oc, KA), f32),
            pltpu.VMEM((3, 2, Y, oc, KA), bf16),
            pltpu.VMEM((3, Y, oc, KA), bf16),
            pltpu.VMEM((3, Y, oc, KA), f32),
            pltpu.VMEM((3, Y, oc, KA), bf16),
            pltpu.VMEM((3, Y, oc, KA), bf16),
            pltpu.VMEM((oc, KC + KTP + 128), f32),
            pltpu.VMEM((T, oc, KTP), f32),
            pltpu.VMEM((T, oc, KTP), bf16),
            pltpu.VMEM((T, oc, KTP), bf16),
            pltpu.VMEM((8, C), f32),
            pltpu.VMEM((S, 8, C), f32),
            pltpu.VMEM((8, C), f32),
            pltpu.VMEM((T, 8, C), f32),
            dma((3,)), dma((5,)), dma((5,)), dma((T,)), dma((T,)),
            dma((S,)), dma((S,)), dma((T,)), dma((T,)),
            dma((3,)), dma((3,)), dma((3, Y)), dma((3, Y)), dma((T,)), dma((T,)),
        ],
        compiler_params=pltpu.CompilerParams(
            collective_id=0, has_side_effects=True, vmem_limit_bytes=56 * 1024 * 1024
        ),
    )(frames, conv_weight, conv_bias.reshape(1, C), projection, levels, centres, code_grad)
    latent_count = levels.shape[0]
    return quantized, wg[:, :KT].T, small[:latent_count].T, small[latent_count]


def solution(mesh):
    return jax.shard_map(
        functools.partial(on_device, mesh.shape["tm"], mesh.shape["space"]),
        mesh=mesh,
        in_specs=(
            P("tm", "space", None, None),
            P(),
            P(),
            P(),
            P(),
            P(None, "space", "tm"),
            P(None, "space", "tm"),
        ),
        out_specs=(P(None, "space", "tm"), P("tm", "space"), P(), P()),
        check_vma=False,
    )
```

time: 199 us -> 41.4 us (0.21); the launches traced: 195 us -> 41.2 us
  waiting for transfers between devices: 71.8 us -> 0 us
  blocking collectives: 47.7 us -> 0 us
  Pallas kernels: 0 us -> 35.9 us
  matrix products: 21.2 us -> 0 us
  local copies, waits for them, and re-layouts: 22.2 us -> 4.62 us
  between operations: 14.4 us -> 0.66 us
  starting transfers between devices: 11.2 us -> 0 us
  other arithmetic: 7.03 us -> 0 us
    psum x1 -> x0, blocking collectives: 38.7 us -> none  [on_device(): lax.psum((projection_part, bias_part), ('tm', 'space'))]
    pallas_call x0 -> x1, Pallas kernels: none -> 35.9 us  [on_device(): pl.pallas_call(functools.partial(block_kernel, T, S, scale), out_shape=(j...]
    unnamed x3 -> x0, waiting for transfers between devices: 31.8 us -> none
    reduce_scatter x1 -> x0, waiting for transfers between devices: 26.6 us -> none  [on_device(): lax.psum_scatter(column_part, 'tm', scatter_dimension=0, tiled=True)]
    dot_general x21 -> x0, matrix products: 21.2 us -> none  [the longest x9 11.7 us: on_device(): lax.dot_general(tap_slab, low_grad, (((0,), (0,)), ((), ())), preferred_e...]
    unnamed x51 -> x6, local copies, waits for them, and re-layouts: 12.4 us -> 2.04 us
    ppermute x3 -> x0, waiting for transfers between devices: 10.3 us -> none  [the longest x1 6.51 us: passed_along(): lax.ppermute(value, axis, [(source, source + steps) for source in range(f...]
    all_to_all x1 -> x0, blocking collectives: 8.94 us -> none  [on_device(): lax.all_to_all(tile_step, 'tm', split_axis=0, concat_axis=2, tiled=True)]
  transfers between devices with their start and end apart: 6 -> 0, of which waited for: 5 -> 0; matrix products, arithmetic and copies ran while one was open for 1% -> 0% of each run, Pallas kernels for 0% -> 0%
where the time goes in v1:
time: 41.4 us; the launch traced here: 41.2 us
  Pallas kernels  35.9 us (87%)
  local copies, waits for them, and re-layouts  4.62 us (11%)
  between operations  0.66 us (2%)
    pallas_call x1, Pallas kernels, on_device(): pl.pallas_call(functools.partial(block_kernel, T, S, scale), out_shape=(j...  35.9 us
    unnamed x6, local copies, waits for them, and re-layouts  2.04 us
    transpose x1, local copies, waits for them, and re-layouts, on_device(): wg[:, :KT]  1.48 us

profile of v1, /device:TPU:24, one launch (start us, length us, event | category | flops | bytes accessed | tf_op | source)
XLA Modules:
  0.0 41.2 jit_solution(15985592272463362123)
XLA Ops:
  0.6 1.4 %copy.11.proj = f32[128,6]{1,0:T(8,128)} copy(f32[128,6]{0,1:T(8,128)} %param.10) | data formatting | bytes 6144 | tf_op args[3]
  2.1 35.9 %shard_map.102 = (f32[8,4,96]{2,1,0:T(4,128)}, f32[32,512]{1,0:T(8,128)}, f32[8,128]{1,0:T(8,128)}) custom-call(bf16[4,4,128,128]{3,2,1,0:T(8,128)(2,1)} %frames.1, bf16[3456,128]{1,0:T(8,128)(2,1)} %weight.1, f32[1,128]{1,0:T(1,128)} %bitcast.7, f32[128,6]{1,0:T(8,128)} %copy.11.proj, s32[6]{0:T(128)} %levels.1, s32[8,4,96]{2,1,0:T(4,128)} %centres.1, ...), custom_call_target="tpu_custom_call" | custom-call | tf_op jit(solution)/shard_map/pallas_call | solution.py:358
  38.0 0.0 copy-start.1
  38.0 0.0 copy-start
  38.0 1.5 %slice_bitcast_fusion = f32[432,32]{0,1:T(8,128)} fusion(f32[32,512]{1,0:T(8,128)} %get-tuple-element.8), kind=kLoop, calls=%fused_computation | loop fusion | bytes 110592 | tf_op jit(solution)/shard_map/transpose | solution.py:400
  39.5 0.0 copy-done.1
  39.5 0.6 %slice_bitcast_fusion.1 = f32[128,6]{0,1:T(8,128)} fusion(f32[8,128]{1,0:T(8,128)S(1)} %copy-done.1), kind=kLoop, calls=%fused_computation.1 | loop fusion | bytes 6144 | tf_op jit(solution)/shard_map/transpose | solution.py:400
  40.1 0.5 %slice_bitcast_fusion.2 = f32[128]{0:T(128)} fusion(f32[8,128]{1,0:T(8,128)S(1)} %copy-done.1), kind=kLoop, calls=%fused_computation.2 | loop fusion | bytes 1024 | tf_op jit(solution)/shard_map/squeeze | solution.py:400
  40.6 0.0 copy-done
  40.6 0.6 %copy.13 = f32[8,4,96]{2,1,0:T(4,128)} copy(f32[8,4,96]{2,1,0:T(4,128)S(1)} %copy-done) | data formatting | bytes 24576
Async XLA Ops:
  38.0 1.5 %copy-start.1 = (f32[8,128]{1,0:T(8,128)S(1)}, f32[8,128]{1,0:T(8,128)}, u32[]{:S(2)}) copy-start(f32[8,128]{1,0:T(8,128)} %get-tuple-element.9) | copy-start | bytes 12292
  38.0 2.6 %copy-start = (f32[8,4,96]{2,1,0:T(4,128)S(1)}, f32[8,4,96]{2,1,0:T(4,128)}, u32[]{:S(2)}) copy-start(f32[8,4,96]{2,1,0:T(4,128)} %get-tuple-element.14) | copy-start | bytes 36868

commit v2 on v1

--- a/solution.py
+++ b/solution.py
@@ -12,6 +12,7 @@
 highest = lax.Precision.HIGHEST
 MESH = pl.DeviceIdType.MESH
 f32, bf16 = jnp.float32, jnp.bfloat16
+core_type, row_type, time_type = f32, bf16, bf16
 
 
 def dot(a, b, ca, cb, precision=None):
@@ -30,7 +31,7 @@
 def block_kernel(
     T, S, scale,
     frames, weight, bias, proj, levels, centres, code_grad,
-    quant_out, weight_out, small_out,
+    quant_out, weight_out, proj_out, bias_out,
     xb, cg_send, cg_recv, pscr, slope_t, gt, acc, stage1, recv1, sum2, stage2, recv2,
     total, own3, stage3, recv3, sm_send, sm_recv, st_send, st_recv,
     local_sem, halo_s, halo_r, cg_s, cg_r, ss_s, ss_r, ts_s, ts_r,
@@ -81,9 +82,6 @@
     cg_send[...] = jnp.zeros_like(cg_send)
     cg_send[:, 0:R, 0:TILE] = code_grad[...]
 
-    def diag(cond, dt, ds):
-        return jnp.where(cond, 1, 0)
-
     n_t = jnp.where(up_t, 1, 0) + jnp.where(dn_t, 1, 0)
     n_s = jnp.where(up_s, 1, 0) + jnp.where(dn_s, 1, 0)
     pl.semaphore_wait(barrier, (S - 1) + (T - 1) + n_t * n_s)
@@ -140,8 +138,8 @@
     quant_out[...] = (centres[...].astype(f32) - half3) / half3
 
     pscr[...] = jnp.zeros_like(pscr)
-    pscr[:, 0:L] = proj[...]
-    proj_t = pscr[...].T[0:8]
+    pscr[0:L] = proj[...]
+    proj_t = pscr[...]
 
     @pl.when(s == 0)
     def _():
@@ -222,7 +220,7 @@
         * scale
     )
     proj_part = dot(step, pooled, 1, 0, highest)
-    pg_t = dot(pscr[:, 0:8], step, 1, 0, highest) * 0.25
+    pg_t = dot(proj_t, step, 0, 0, highest) * 0.25
 
     lane = lax.broadcasted_iota(jnp.int32, (C, W), 1)
     bias_sum = jnp.zeros((C, W), f32)
@@ -267,7 +265,7 @@
                 for sp in range(S):
                     blk = res[c * C + sp * oc : c * C + (sp + 1) * oc, b * C : (b + 1) * C]
                     acc[a, sp % 2, sp // 2, :, k0 : k0 + C] = blk
-                    stage1[a, sp % 2, sp // 2, :, k0 : k0 + C] = blk.astype(bf16)
+                    stage1[a, sp % 2, sp // 2, :, k0 : k0 + C] = blk.astype(core_type)
         core_copy(a).start()
 
     def fold_core(a):
@@ -275,7 +273,7 @@
         for yy in range(Y):
             v = acc[a, core, yy] + recv1[a, yy].astype(f32)
             sum2[a, yy] = v
-            stage2[a, yy] = v.astype(bf16)
+            stage2[a, yy] = v.astype(row_type)
         for d in range(1, Y):
             y_copy(a, d).start()
 
@@ -296,7 +294,7 @@
                 win = pltpu.roll(win, KTP + 128 - (off - base), 1)
             win = win[:, 0:KTP]
             own3[to] = win
-            stage3[to] = win.astype(bf16)
+            stage3[to] = win.astype(time_type)
             start_if(t != to, tm_copy(to, t))
             done[0] += 1
 
@@ -321,14 +319,15 @@
     for d in range(1, T):
         small_time(d).wait_recv()
         sm = sm + st_recv[d]
-    small_out[...] = sm
+    proj_out[...] = sm[0:L]
+    bias_out[...] = sm[L : L + 1]
 
     res = own3[t]
     for d in range(1, T):
         src = lax.rem(t + d, T)
         tm_copy(src, src).wait_recv()
         res = res + recv3[src].astype(f32)
-    weight_out[...] = res
+    weight_out[...] = res[:, 0:KT]
 
     for sends, _, copy in halos:
         sent_if(sends, copy)
@@ -355,35 +354,36 @@
     vmem = pl.BlockSpec(memory_space=pltpu.VMEM)
     dma = pltpu.SemaphoreType.DMA
     KA = KC // 3
-    quantized, wg, small = pl.pallas_call(
+    quantized, wg, proj_grad, bias_grad = pl.pallas_call(
         functools.partial(block_kernel, T, S, scale),
         out_shape=(
             jax.ShapeDtypeStruct(centres.shape, f32),
-            jax.ShapeDtypeStruct((oc, KTP), f32),
-            jax.ShapeDtypeStruct((8, C), f32),
+            jax.ShapeDtypeStruct((oc, KT), f32),
+            jax.ShapeDtypeStruct((levels.shape[0], C), f32),
+            jax.ShapeDtypeStruct((1, C), f32),
         ),
         in_specs=[
             pl.BlockSpec(memory_space=pl.ANY), vmem, vmem, vmem,
             pl.BlockSpec(memory_space=pltpu.SMEM), vmem, vmem,
         ],
-        out_specs=(vmem, vmem, vmem),
+        out_specs=(vmem,) * 4,
         scratch_shapes=[
             pltpu.VMEM((F + 2, R + 2, W, C), bf16),
             pltpu.VMEM((T, 8, 128), f32),
             pltpu.VMEM((T, 8, 128), f32),
-            pltpu.VMEM((C, C), f32),
+            pltpu.VMEM((8, C), f32),
             pltpu.VMEM((F * R, C, W), f32),
             pltpu.VMEM((3 * C, F * cells), bf16),
             pltpu.VMEM((3, 2, Y, oc, KA), f32),
-            pltpu.VMEM((3, 2, Y, oc, KA), bf16),
-            pltpu.VMEM((3, Y, oc, KA), bf16),
+            pltpu.VMEM((3, 2, Y, oc, KA), core_type),
+            pltpu.VMEM((3, Y, oc, KA), core_type),
             pltpu.VMEM((3, Y, oc, KA), f32),
-            pltpu.VMEM((3, Y, oc, KA), bf16),
-            pltpu.VMEM((3, Y, oc, KA), bf16),
+            pltpu.VMEM((3, Y, oc, KA), row_type),
+            pltpu.VMEM((3, Y, oc, KA), row_type),
             pltpu.VMEM((oc, KC + KTP + 128), f32),
             pltpu.VMEM((T, oc, KTP), f32),
-            pltpu.VMEM((T, oc, KTP), bf16),
-            pltpu.VMEM((T, oc, KTP), bf16),
+            pltpu.VMEM((T, oc, KTP), time_type),
+            pltpu.VMEM((T, oc, KTP), time_type),
             pltpu.VMEM((8, C), f32),
             pltpu.VMEM((S, 8, C), f32),
             pltpu.VMEM((8, C), f32),
@@ -395,9 +395,8 @@
         compiler_params=pltpu.CompilerParams(
             collective_id=0, has_side_effects=True, vmem_limit_bytes=56 * 1024 * 1024
         ),
-    )(frames, conv_weight, conv_bias.reshape(1, C), projection, levels, centres, code_grad)
-    latent_count = levels.shape[0]
-    return quantized, wg[:, :KT].T, small[:latent_count].T, small[latent_count]
+    )(frames, conv_weight, conv_bias.reshape(1, C), projection.T, levels, centres, code_grad)
+    return quantized, wg.T, proj_grad.T, bias_grad.reshape(C)
 
 
 def solution(mesh):

time: 41.4 us -> 40.7 us (0.983)
  local copies, waits for them, and re-layouts: 4.62 us -> 3.98 us
    transpose x2 -> x0, local copies, waits for them, and re-layouts: 2.07 us -> none  [the longest x1 1.48 us: on_device(): wg[:, :KT]]
    unnamed x6 -> x8, local copies, waits for them, and re-layouts: 2.04 us -> 3.98 us
    squeeze x1 -> x0, local copies, waits for them, and re-layouts: 0.51 us -> none  [on_device(): small[latent_count]]
where the time goes in v2:
time: 40.7 us; the launch traced here: 40.5 us
  Pallas kernels  35.9 us (88%)
  local copies, waits for them, and re-layouts  3.98 us (10%)
  between operations  0.64 us (2%)
    pallas_call x1, Pallas kernels, on_device(): pl.pallas_call(functools.partial(block_kernel, T, S, scale), out_shape=(j...  35.9 us
    unnamed x8, local copies, waits for them, and re-layouts  3.98 us

profile of v2, /device:TPU:24, one launch (start us, length us, event | category | flops | bytes accessed | tf_op | source)
XLA Modules:
  0.0 40.5 jit_solution(9861633960205633357)
XLA Ops:
  0.6 35.9 %shard_map.102 = (f32[8,4,96]{2,1,0:T(4,128)}, f32[32,432]{1,0:T(8,128)}, f32[6,128]{1,0:T(8,128)}, f32[1,128]{1,0:T(1,128)}) custom-call(bf16[4,4,128,128]{3,2,1,0:T(8,128)(2,1)} %frames.1, bf16[3456,128]{1,0:T(8,128)(2,1)} %weight.1, f32[1,128]{1,0:T(1,128)} %bitcast.8, f32[6,128]{1,0:T(8,128)} %bitcast.6, s32[6]{0:T(128)} %levels.1, s32[8,4,96]{2,1,0:T(4,128)} %centres.1, ...), custom_call_target="tpu_custom_call" | custom-call | tf_op jit(solution)/shard_map/pallas_call | solution.py:357
  36.5 1.3 %copy.15 = f32[8,4,96]{2,1,0:T(4,128)} copy(f32[8,4,96]{2,1,0:T(4,128)} %get-tuple-element.16) | data formatting | bytes 24576
  37.8 0.0 copy-start
  37.8 1.5 %copy.16 = f32[432,32]{0,1:T(8,128)} copy(f32[432,32]{0,1:T(8,128)} %bitcast.5) | data formatting | bytes 110592
  39.3 0.0 copy-done
  39.3 0.0 copy-start.1
  39.3 0.6 %copy.17 = f32[128,6]{0,1:T(8,128)} copy(f32[128,6]{0,1:T(8,128)S(1)} %bitcast.7) | data formatting | bytes 6144
  39.9 0.1 copy-done.1
  40.0 0.5 %copy.18 = f32[128]{0:T(128)} copy(f32[128]{0:T(128)S(1)} %bitcast.9) | data formatting | bytes 1024
Async XLA Ops:
  37.8 1.5 %copy-start = (f32[6,128]{1,0:T(8,128)S(1)}, f32[6,128]{1,0:T(8,128)}, u32[]{:S(2)}) copy-start(f32[6,128]{1,0:T(8,128)} %get-tuple-element.10) | copy-start | bytes 9220
  39.3 0.7 %copy-start.1 = (f32[1,128]{1,0:T(1,128)S(1)}, f32[1,128]{1,0:T(1,128)}, u32[]{:S(2)}) copy-start(f32[1,128]{1,0:T(1,128)} %get-tuple-element.11) | copy-start | bytes 1540

commit v3 on v2

--- a/solution.py
+++ b/solution.py
@@ -34,7 +34,7 @@
     quant_out, weight_out, proj_out, bias_out,
     xb, cg_send, cg_recv, pscr, slope_t, gt, acc, stage1, recv1, sum2, stage2, recv2,
     total, own3, stage3, recv3, sm_send, sm_recv, st_send, st_recv,
-    local_sem, halo_s, halo_r, cg_s, cg_r, ss_s, ss_r, ts_s, ts_r,
+    local_sem, halo_s, halo_r, corner_s, corner_r, cg_s, cg_r, ss_s, ss_r, ts_s, ts_r,
     core_s, core_r, y_s, y_r, tm_s, tm_r,
 ):
     Y = S // 2
@@ -61,12 +61,6 @@
         signal(t, lax.rem(s + d, S))
     for d in range(1, T):
         signal(lax.rem(t + d, T), s)
-    for ct, dt in ((up_t, 1), (dn_t, -1)):
-        for cs_, ds in ((up_s, 1), (dn_s, -1)):
-            @pl.when(jnp.logical_and(ct, cs_))
-            def _():
-                signal(t + dt, s + ds)
-
     own = pltpu.make_async_copy(frames, xb.at[2 : 2 + F, 1 : 1 + R], local_sem.at[0])
     own.start()
     first = [
@@ -82,9 +76,7 @@
     cg_send[...] = jnp.zeros_like(cg_send)
     cg_send[:, 0:R, 0:TILE] = code_grad[...]
 
-    n_t = jnp.where(up_t, 1, 0) + jnp.where(dn_t, 1, 0)
-    n_s = jnp.where(up_s, 1, 0) + jnp.where(dn_s, 1, 0)
-    pl.semaphore_wait(barrier, (S - 1) + (T - 1) + n_t * n_s)
+    pl.semaphore_wait(barrier, (S - 1) + (T - 1))
 
     def remote(src, dst, ss_, rs_, tt, sp):
         return pltpu.make_async_remote_copy(
@@ -98,14 +90,10 @@
                             halo_s.at[0], halo_r.at[0], t, s + 1)),
         (dn_s, up_s, remote(frames.at[:, 0], xb.at[2 : 2 + F, H],
                             halo_s.at[1], halo_r.at[1], t, s - 1)),
-        (up_t, dn_t, remote(frames.at[F - 2 : F], xb.at[0:2, 1:H],
+        (up_t, dn_t, remote(frames.at[F - 1], xb.at[1, 1:H],
                             halo_s.at[2], halo_r.at[2], t + 1, s)),
-        (jnp.logical_and(up_t, up_s), jnp.logical_and(dn_t, dn_s),
-         remote(frames.at[F - 2 : F, R - 1], xb.at[0:2, 0],
-                halo_s.at[3], halo_r.at[3], t + 1, s + 1)),
-        (jnp.logical_and(up_t, dn_s), jnp.logical_and(dn_t, up_s),
-         remote(frames.at[F - 2 : F, 0], xb.at[0:2, H],
-                halo_s.at[4], halo_r.at[4], t + 1, s - 1)),
+        (up_t, dn_t, remote(frames.at[F - 2], xb.at[0, 1:H],
+                            halo_s.at[3], halo_r.at[3], t + 1, s)),
     ]
 
     def start_if(cond, copy):
@@ -125,6 +113,22 @@
 
     for sends, _, copy in halos:
         start_if(sends, copy)
+
+    corners = [
+        [
+            (jnp.logical_and(dn_t, up_s), jnp.logical_and(dn_t, dn_s),
+             remote(xb.at[k, R], xb.at[k, 0], corner_s.at[2 * k], corner_r.at[2 * k], t, s + 1)),
+            (jnp.logical_and(dn_t, dn_s), jnp.logical_and(dn_t, up_s),
+             remote(xb.at[k, 1], xb.at[k, H], corner_s.at[2 * k + 1], corner_r.at[2 * k + 1], t, s - 1)),
+        ]
+        for k in range(2)
+    ]
+
+    def pass_corners(k):
+        _, gets, copy = halos[3 - k]
+        recv_if(gets, copy)
+        for sends, _, corner in corners[k]:
+            start_if(sends, corner)
 
     def cg_copy(d):
         to = lax.rem(t + d, T)
@@ -177,9 +181,6 @@
         recv_if(gets, copy)
     pooled = conv_frame(2) + conv_frame(3)
 
-    for _, gets, copy in halos[2:]:
-        recv_if(gets, copy)
-
     @pl.when(t == 0)
     def _():
         for k in range(2):
@@ -187,7 +188,11 @@
             xb[k, 0] = xb[2, 0]
             xb[k, H] = xb[2, H]
 
-    pooled = (pooled + conv_frame(0) + conv_frame(1)) * 0.25
+    pass_corners(1)
+    for _, gets, copy in corners[1]:
+        recv_if(gets, copy)
+    pooled = pooled + conv_frame(1)
+    pass_corners(0)
 
     for d in range(1, T):
         cg_copy(d).wait_recv()
@@ -210,6 +215,10 @@
     fold = jnp.logical_and(m_i % L == j_i, m_i < TILE).astype(f32)
     code = dot(fold, spread, 1, 0, highest)
 
+    for _, gets, copy in corners[0]:
+        recv_if(gets, copy)
+    pooled = (pooled + conv_frame(0)) * 0.25
+
     latent = dot(proj_t, pooled, 1, 1, highest)
     squashed = jnp.tanh(latent)
     half_j = per_level(levels, lax.broadcasted_iota(jnp.int32, (8, cells), 0), L)
@@ -277,7 +286,7 @@
         for d in range(1, Y):
             y_copy(a, d).start()
 
-    done = [0]
+    folded, sent = set(), set()
 
     def fold_y(a):
         v = sum2[a, y]
@@ -285,9 +294,12 @@
             y_copy(a, d).wait_recv()
             v = v + recv2[a, d].astype(f32)
         total[:, a * KA : (a + 1) * KA] = v
-        while (done[0] + 1) * KT <= (a + 1) * KA:
-            to = done[0]
+        folded.add(a)
+        for to in range(T):
             off = to * KT
+            if to in sent or not {off // KA, (off + KT - 1) // KA} <= folded:
+                continue
+            sent.add(to)
             base = off // 128 * 128
             win = total[:, base : base + KTP + 128]
             if off > base:
@@ -296,9 +308,8 @@
             own3[to] = win
             stage3[to] = win.astype(time_type)
             start_if(t != to, tm_copy(to, t))
-            done[0] += 1
-
-    total[:, KC:] = jnp.zeros((oc, total.shape[1] - KC), f32)
+
+    total[...] = jnp.zeros(total.shape, f32)
     products(0)
     sm = sm_send[...]
     for d in range(1, S):
@@ -307,14 +318,14 @@
     st_send[...] = sm
     for d in range(1, T):
         small_time(d).start()
+    products(2)
+    fold_core(0)
     products(1)
-    fold_core(0)
-    products(2)
+    fold_core(2)
+    fold_y(0)
     fold_core(1)
-    fold_y(0)
-    fold_core(2)
+    fold_y(2)
     fold_y(1)
-    fold_y(2)
 
     for d in range(1, T):
         small_time(d).wait_recv()
@@ -329,7 +340,7 @@
         res = res + recv3[src].astype(f32)
     weight_out[...] = res[:, 0:KT]
 
-    for sends, _, copy in halos:
+    for sends, _, copy in halos + corners[0] + corners[1]:
         sent_if(sends, copy)
     for d in range(1, T):
         cg_copy(d).wait_send()
@@ -388,7 +399,7 @@
             pltpu.VMEM((S, 8, C), f32),
             pltpu.VMEM((8, C), f32),
             pltpu.VMEM((T, 8, C), f32),
-            dma((3,)), dma((5,)), dma((5,)), dma((T,)), dma((T,)),
+            dma((3,)), dma((4,)), dma((4,)), dma((4,)), dma((4,)), dma((T,)), dma((T,)),
             dma((S,)), dma((S,)), dma((T,)), dma((T,)),
             dma((3,)), dma((3,)), dma((3, Y)), dma((3, Y)), dma((T,)), dma((T,)),
         ],

time: 40.7 us -> 40.9 us (level)
  the two profiles are of different devices: /device:TPU:24 before, /device:TPU:20 now
where the time goes in v3:
time: 40.9 us; the launch traced here: 40.7 us
  Pallas kernels  36 us (88%)
  local copies, waits for them, and re-layouts  3.98 us (10%)
  between operations  0.64 us (2%)
    pallas_call x1, Pallas kernels, on_device(): pl.pallas_call(functools.partial(block_kernel, T, S, scale), out_shape=(j...  36 us
    unnamed x8, local copies, waits for them, and re-layouts  3.98 us

profile of v3, /device:TPU:20, one launch (start us, length us, event | category | flops | bytes accessed | tf_op | source)
XLA Modules:
  0.0 40.7 jit_solution(2942086098184267568)
XLA Ops:
  0.6 36.0 %shard_map.102 = (f32[8,4,96]{2,1,0:T(4,128)}, f32[32,432]{1,0:T(8,128)}, f32[6,128]{1,0:T(8,128)}, f32[1,128]{1,0:T(1,128)}) custom-call(bf16[4,4,128,128]{3,2,1,0:T(8,128)(2,1)} %frames.1, bf16[3456,128]{1,0:T(8,128)(2,1)} %weight.1, f32[1,128]{1,0:T(1,128)} %bitcast.8, f32[6,128]{1,0:T(8,128)} %bitcast.6, s32[6]{0:T(128)} %levels.1, s32[8,4,96]{2,1,0:T(4,128)} %centres.1, ...), custom_call_target="tpu_custom_call" | custom-call | tf_op jit(solution)/shard_map/pallas_call | solution.py:368
  36.7 1.3 %copy.15 = f32[8,4,96]{2,1,0:T(4,128)} copy(f32[8,4,96]{2,1,0:T(4,128)} %get-tuple-element.16) | data formatting | bytes 24576
  38.0 0.0 copy-start
  38.0 1.5 %copy.16 = f32[432,32]{0,1:T(8,128)} copy(f32[432,32]{0,1:T(8,128)} %bitcast.5) | data formatting | bytes 110592
  39.5 0.0 copy-done
  39.5 0.0 copy-start.1
  39.5 0.6 %copy.17 = f32[128,6]{0,1:T(8,128)} copy(f32[128,6]{0,1:T(8,128)S(1)} %bitcast.7) | data formatting | bytes 6144
  40.1 0.1 copy-done.1
  40.2 0.5 %copy.18 = f32[128]{0:T(128)} copy(f32[128]{0:T(128)S(1)} %bitcast.9) | data formatting | bytes 1024
Async XLA Ops:
  38.0 1.5 %copy-start = (f32[6,128]{1,0:T(8,128)S(1)}, f32[6,128]{1,0:T(8,128)}, u32[]{:S(2)}) copy-start(f32[6,128]{1,0:T(8,128)} %get-tuple-element.10) | copy-start | bytes 9220
  39.5 0.7 %copy-start.1 = (f32[1,128]{1,0:T(1,128)S(1)}, f32[1,128]{1,0:T(1,128)}, u32[]{:S(2)}) copy-start(f32[1,128]{1,0:T(1,128)} %get-tuple-element.11) | copy-start | bytes 1540

commit v4 on v2

--- a/solution.py
+++ b/solution.py
@@ -30,8 +30,8 @@
 
 def block_kernel(
     T, S, scale,
-    frames, weight, bias, proj, levels, centres, code_grad,
-    quant_out, weight_out, proj_out, bias_out,
+    frames, weight, bias, proj, levels, code_grad,
+    weight_out, small_out,
     xb, cg_send, cg_recv, pscr, slope_t, gt, acc, stage1, recv1, sum2, stage2, recv2,
     total, own3, stage3, recv3, sm_send, sm_recv, st_send, st_recv,
     local_sem, halo_s, halo_r, cg_s, cg_r, ss_s, ss_r, ts_s, ts_r,
@@ -132,10 +132,6 @@
 
     for d in range(1, T):
         cg_copy(d).start()
-
-    lane3 = lax.broadcasted_iota(jnp.int32, centres.shape, 2)
-    half3 = per_level(levels, lax.rem(lane3, L), L)
-    quant_out[...] = (centres[...].astype(f32) - half3) / half3
 
     pscr[...] = jnp.zeros_like(pscr)
     pscr[0:L] = proj[...]
@@ -319,8 +315,7 @@
     for d in range(1, T):
         small_time(d).wait_recv()
         sm = sm + st_recv[d]
-    proj_out[...] = sm[0:L]
-    bias_out[...] = sm[L : L + 1]
+    small_out[...] = sm
 
     res = own3[t]
     for d in range(1, T):
@@ -344,6 +339,16 @@
         sent_if(t != to, tm_copy(to, t))
 
 
+def finish_kernel(levels, centres, wg, small, quant_out, weight_out, proj_out, bias_out):
+    L = levels.shape[0]
+    lane = lax.broadcasted_iota(jnp.int32, centres.shape, 2)
+    half = per_level(levels, lax.rem(lane, L), L)
+    quant_out[...] = (centres[...].astype(f32) - half) / half
+    weight_out[...] = wg[...]
+    proj_out[...] = small[0:L]
+    bias_out[...] = small[L : L + 1]
+
+
 def on_device(T, S, frames, conv_weight, conv_bias, projection, levels, centres, code_grad):
     F, R, W, C = frames.shape
     KC = conv_weight.shape[0]
@@ -354,19 +359,17 @@
     vmem = pl.BlockSpec(memory_space=pltpu.VMEM)
     dma = pltpu.SemaphoreType.DMA
     KA = KC // 3
-    quantized, wg, proj_grad, bias_grad = pl.pallas_call(
+    wg, small = pl.pallas_call(
         functools.partial(block_kernel, T, S, scale),
         out_shape=(
-            jax.ShapeDtypeStruct(centres.shape, f32),
             jax.ShapeDtypeStruct((oc, KT), f32),
-            jax.ShapeDtypeStruct((levels.shape[0], C), f32),
-            jax.ShapeDtypeStruct((1, C), f32),
+            jax.ShapeDtypeStruct((8, C), f32),
         ),
         in_specs=[
             pl.BlockSpec(memory_space=pl.ANY), vmem, vmem, vmem,
-            pl.BlockSpec(memory_space=pltpu.SMEM), vmem, vmem,
+            pl.BlockSpec(memory_space=pltpu.SMEM), vmem,
         ],
-        out_specs=(vmem,) * 4,
+        out_specs=(vmem, vmem),
         scratch_shapes=[
             pltpu.VMEM((F + 2, R + 2, W, C), bf16),
             pltpu.VMEM((T, 8, 128), f32),
@@ -395,7 +398,19 @@
         compiler_params=pltpu.CompilerParams(
             collective_id=0, has_side_effects=True, vmem_limit_bytes=56 * 1024 * 1024
         ),
-    )(frames, conv_weight, conv_bias.reshape(1, C), projection.T, levels, centres, code_grad)
+    )(frames, conv_weight, conv_bias.reshape(1, C), projection.T, levels, code_grad)
+    L = levels.shape[0]
+    quantized, wg, proj_grad, bias_grad = pl.pallas_call(
+        finish_kernel,
+        out_shape=(
+            jax.ShapeDtypeStruct(centres.shape, f32),
+            jax.ShapeDtypeStruct(wg.shape, f32),
+            jax.ShapeDtypeStruct((L, C), f32),
+            jax.ShapeDtypeStruct((1, C), f32),
+        ),
+        in_specs=[pl.BlockSpec(memory_space=pltpu.SMEM), vmem, vmem, vmem],
+        out_specs=(vmem,) * 4,
+    )(levels, centres, wg, small)
     return quantized, wg.T, proj_grad.T, bias_grad.reshape(C)
 
 

time: 40.7 us -> 38.2 us (0.939)
  local copies, waits for them, and re-layouts: 3.98 us -> 0 us
  Pallas kernels: 35.9 us -> 37.3 us
    unnamed x8 -> x0, local copies, waits for them, and re-layouts: 3.98 us -> none
    pallas_call x0 -> x1, Pallas kernels: none -> 1.5 us  [on_device(): pl.pallas_call(finish_kernel, out_shape=(jax.ShapeDtypeStruct(centres.sha...]
where the time goes in v4:
time: 38.2 us; the launch traced here: 38 us
  Pallas kernels  37.3 us (98%)
  between operations  0.64 us (2%)
    pallas_call x1, Pallas kernels, on_device(): pl.pallas_call(functools.partial(block_kernel, T, S, scale), out_shape=(j...  35.8 us
    pallas_call x1, Pallas kernels, on_device(): pl.pallas_call(finish_kernel, out_shape=(jax.ShapeDtypeStruct(centres.sha...  1.5 us

profile of v4, /device:TPU:24, one launch (start us, length us, event | category | flops | bytes accessed | tf_op | source)
XLA Modules:
  0.0 38.0 jit_solution(15323667700094521630)
XLA Ops:
  0.6 35.8 %shard_map.102 = (f32[32,432]{1,0:T(8,128)}, f32[8,128]{1,0:T(8,128)}) custom-call(bf16[4,4,128,128]{3,2,1,0:T(8,128)(2,1)} %frames.1, bf16[3456,128]{1,0:T(8,128)(2,1)} %weight.1, f32[1,128]{1,0:T(1,128)} %bitcast.6, f32[6,128]{1,0:T(8,128)} %bitcast.5, s32[6]{0:T(128)} %levels.3, f32[8,4,96]{2,1,0:T(4,128)} %code_grad.1), custom_call_target="tpu_custom_call" | custom-call | tf_op jit(solution)/shard_map/pallas_call | solution.py:362
  36.5 1.5 %shard_map.103 = (f32[8,4,96]{2,1,0:T(4,128)}, f32[32,432]{1,0:T(8,128)}, f32[6,128]{1,0:T(8,128)}, f32[1,128]{1,0:T(1,128)}) custom-call(s32[6]{0:T(128)} %levels.3, s32[8,4,96]{2,1,0:T(4,128)} %centres.1, f32[32,432]{1,0:T(8,128)} %get-tuple-element.10.wg, f32[8,128]{1,0:T(8,128)} %get-tuple-element.11.small), custom_call_target="tpu_custom_call" | custom-call | tf_op jit(solution)/shard_map/pallas_call | solution.py:403
